TPU v7x, 32 devices: a whole 2x2x4 slice. The times are simulated.
32 devices in a mesh: rows: 16 (over z, y, x), cols: 2 (over core).
Axes of the slice: x: 2, y: 2, z: 4, core: 2. Of those that a mesh axis runs over, the one named last changes fastest.
Arguments:
- tokens_in: bfloat16 [6304, 768], P(('rows', 'cols')), may hold values from -6 to 6
- ln1_gain: float32 [768], replicated, may hold values from 0.5 to 1.5
- ln1_shift: float32 [768], replicated, may hold values from -4 to 4
- qkv_weight: bfloat16 [768, 2304], P(None, 'cols'), may hold values from -0.21875 to 0.21875
- out_weight: bfloat16 [768, 768], P('cols'), may hold values from -1.75 to 1.75
- ln2_gain: float32 [768], replicated, may hold values from 0.5 to 1.5
- ln2_shift: float32 [768], replicated, may hold values from -4 to 4
- router_weight: bfloat16 [768, 32], replicated, may hold values from -0.4375 to 0.4375
- expert_in: bfloat16 [768, 98304], P(None, ('rows', 'cols')), may hold values from -0.21875 to 0.21875
- expert_out: bfloat16 [98304, 768], P(('rows', 'cols')), may hold values from -0.4375 to 0.4375
- routes: int32 [6304, 2], P(('rows', 'cols')), may hold values from 0 to 31, all different within a row; in each aligned block of 197 rows (0 to 196, 197 to 393, ...) at most 16 rows name the same one
- cotangent: bfloat16 [6304, 768], P(('rows', 'cols')), may hold values from -6 to 6
Outputs:
- output: bfloat16 [6304, 768], P(('rows', 'cols'))
- tokens_grad: bfloat16 [6304, 768], P(('rows', 'cols'))
- ln1_gain_grad: float32 [768], replicated
- ln1_shift_grad: float32 [768], replicated
- qkv_grad: float32 [768, 2304], P(None, 'cols')
- out_grad: float32 [768, 768], P('cols')
- ln2_gain_grad: float32 [768], replicated
- ln2_shift_grad: float32 [768], replicated
- router_grad: float32 [768, 32], replicated
- expert_in_grad: float32 [768, 98304], P(None, ('rows', 'cols'))
- expert_out_grad: float32 [98304, 768], P(('rows', 'cols'))
Inputs may be any that keep to these rules, and one draw needn't show every extreme that they name: `routes`: the two experts of a token differ. Among the tokens of one device (aligned blocks of 197 rows) each expert is named by at most 16 assignments, a bound that some block reaches.
All inputs are finite; a program needn't handle non-finite values.
Results may differ from a plain program's by a relative error of at most 0.022.
Values may be sent and summed in bfloat16 or wider, within the bound.
A program may use at most 192 MiB of HBM per device.

v0:
```python
import jax
import jax.numpy as jnp
from jax import lax
from jax.sharding import PartitionSpec as P

DH = 64
FF = 3072
SEQ = 197
EPSILON = 1e-06


def layer_norm(values, norm_gain, norm_shift):
    average = jnp.mean(values, axis=-1, keepdims=True)
    centred = values - average
    variance = jnp.mean(centred * centred, axis=-1, keepdims=True)
    return centred * lax.rsqrt(variance + EPSILON) * norm_gain + norm_shift


def gelu_slope(pre_act):
    normal_cdf = 0.5 * (1.0 + jax.scipy.special.erf(pre_act * 0.7071067811865476))
    density = jnp.exp(-0.5 * pre_act * pre_act) * 0.3989422804014327
    return normal_cdf + pre_act * density


def dot_rows(first_side, second_side):
    return lax.dot_general(
        first_side, second_side, (((0,), (0,)), ((), ())), preferred_element_type=jnp.float32
    )


def dot_last(first_side, second_side):
    return lax.dot_general(
        first_side, second_side, (((1,), (1,)), ((), ())), preferred_element_type=jnp.float32
    )


def attention_scores(queries, keys_all, score_scale):
    scores = jnp.einsum("nqhd,nkhd->nhqk", queries, keys_all, preferred_element_type=jnp.float32)
    return scores * score_scale


def body(
    tokens_in,
    ln1_gain,
    ln1_shift,
    qkv_weight,
    out_weight,
    ln2_gain,
    ln2_shift,
    router_weight,
    expert_in,
    expert_out,
    routes,
    cotangent,
):
    local_rows = tokens_in.shape[0]
    model_width = tokens_in.shape[1]
    experts = router_weight.shape[1]
    capacity = max(2, 8 * local_rows // (3 * experts))
    heads_local = qkv_weight.shape[1] // (3 * DH)
    score_scale = DH ** (-0.5)
    row_count = lax.axis_size("rows")
    row_place = lax.axis_index("rows")
    col_place = lax.axis_index("cols")
    per_device = max(1, experts // row_count)
    copies = max(1, row_count // experts)
    slots = per_device * capacity
    piece_half = expert_in.shape[1]
    piece_whole = piece_half * lax.axis_size("cols")
    arrived_rows = row_count * slots
    tokens_f = tokens_in.astype(jnp.float32)
    normed_low = layer_norm(tokens_f, ln1_gain, ln1_shift).astype(jnp.bfloat16)
    gathered = lax.all_gather(normed_low, "cols", axis=0, tiled=True)
    pair_rows = gathered.shape[0]
    images = pair_rows // SEQ
    qkv_low = jnp.dot(gathered, qkv_weight, preferred_element_type=jnp.float32).astype(jnp.bfloat16)
    head_split = qkv_low.reshape(images, SEQ, heads_local, 3, DH)
    queries = head_split[:, :, :, 0]
    keys_all = head_split[:, :, :, 1]
    values_all = head_split[:, :, :, 2]
    scores = attention_scores(queries, keys_all, score_scale)
    score_peak = jnp.max(scores, axis=-1, keepdims=True)
    log_total = score_peak + jnp.log(jnp.sum(jnp.exp(scores - score_peak), axis=-1, keepdims=True))
    weights_low = jnp.exp(scores - log_total).astype(jnp.bfloat16)
    context = jnp.einsum(
        "nhqk,nkhd->nqhd", weights_low, values_all, preferred_element_type=jnp.float32
    )
    context_low = context.astype(jnp.bfloat16).reshape(pair_rows, heads_local * DH)
    row_block = context_low
    attn_out = lax.psum_scatter(
        jnp.dot(row_block, out_weight, preferred_element_type=jnp.float32),
        "cols",
        scatter_dimension=0,
        tiled=True,
    )
    hidden_one = tokens_f + attn_out
    mixed_low = layer_norm(hidden_one, ln2_gain, ln2_shift).astype(jnp.bfloat16)
    logits = jnp.dot(mixed_low, router_weight, preferred_element_type=jnp.float32)
    router_probs = jax.nn.softmax(logits, axis=-1)
    expert_ids = jnp.arange(experts, dtype=jnp.int32)
    chosen = (routes[:, :, None] == expert_ids[None, None, :]).astype(jnp.float32)
    gate_values = jnp.sum(router_probs[:, None, :] * chosen, axis=-1)
    flat_ids = routes.reshape(-1)
    flat_hot = (flat_ids[:, None] == expert_ids[None, :]).astype(jnp.int32)
    slot_ranks = jnp.sum(jnp.cumsum(flat_hot, axis=0) * flat_hot, axis=1) - 1
    first_device = flat_ids // per_device * copies
    slot_index = flat_ids % per_device * capacity + slot_ranks
    copy_ids = jnp.arange(copies, dtype=jnp.int32)
    targets = ((first_device[:, None] + copy_ids[None, :]) * slots + slot_index[:, None]).reshape(
        -1
    )
    grad_out = cotangent.astype(jnp.float32)
    grad_slots = (
        (gate_values[:, :, None] * grad_out[:, None, :])
        .astype(jnp.bfloat16)
        .reshape(2 * local_rows, model_width)
    )
    rows_send = (
        jnp.zeros((arrived_rows, model_width), jnp.bfloat16)
        .at[targets]
        .set(jnp.repeat(mixed_low, 2 * copies, axis=0))
    )
    grads_send = (
        jnp.zeros((arrived_rows, model_width), jnp.bfloat16)
        .at[targets]
        .set(jnp.repeat(grad_slots, copies, axis=0))
    )
    arrived, grad_result = (
        lax.all_to_all(
            rows_send.reshape(row_count, slots, model_width),
            "rows",
            split_axis=0,
            concat_axis=0,
            tiled=True,
        ),
        lax.all_to_all(
            grads_send.reshape(row_count, slots, model_width),
            "rows",
            split_axis=0,
            concat_axis=0,
            tiled=True,
        ),
    )
    arrived = arrived.reshape(arrived_rows, model_width)
    grad_result = grad_result.reshape(arrived_rows, model_width)
    unit_base = row_place % copies * piece_whole
    both_rows, both_grads = (
        lax.all_gather(arrived, "cols", axis=0, tiled=True),
        lax.all_gather(grad_result, "cols", axis=0, tiled=True),
    )
    slot_local = jnp.arange(both_rows.shape[0], dtype=jnp.int32) % slots // capacity
    unit_local = (
        unit_base + col_place * piece_half + jnp.arange(piece_half, dtype=jnp.int32)
    ) // FF
    mask = (slot_local[:, None] == unit_local[None, :]).astype(jnp.float32)
    pre_act = jnp.dot(both_rows, expert_in, preferred_element_type=jnp.float32) * mask
    act_low = jax.nn.gelu(pre_act, approximate=False).astype(jnp.bfloat16)
    result_low = lax.psum_scatter(
        jnp.dot(act_low, expert_out, preferred_element_type=jnp.float32).astype(jnp.bfloat16),
        "cols",
        scatter_dimension=0,
        tiled=True,
    )
    grad_act = dot_last(both_grads, expert_out)
    grad_pre_low = (grad_act * gelu_slope(pre_act) * mask).astype(jnp.bfloat16)
    first_grad = dot_rows(both_rows, grad_pre_low)
    second_grad = dot_rows(act_low, both_grads)
    grad_arrived = lax.psum_scatter(
        dot_last(grad_pre_low, expert_in).astype(jnp.bfloat16),
        "cols",
        scatter_dimension=0,
        tiled=True,
    )
    returned = lax.all_to_all(
        result_low.reshape(row_count, slots, model_width),
        "rows",
        split_axis=0,
        concat_axis=0,
        tiled=True,
    )
    returned = returned.reshape(arrived_rows, model_width)
    picked = jnp.sum(
        returned[targets].reshape(local_rows, 2, copies, model_width).astype(jnp.float32), axis=2
    )
    output = (hidden_one + jnp.sum(gate_values[:, :, None] * picked, axis=1)).astype(jnp.bfloat16)
    grad_gates = jnp.sum(grad_out[:, None, :] * picked, axis=-1)
    grad_sent = lax.all_to_all(
        grad_arrived.reshape(row_count, slots, model_width),
        "rows",
        split_axis=0,
        concat_axis=0,
        tiled=True,
    )
    grad_sent = grad_sent.reshape(arrived_rows, model_width)
    grad_mixed_experts = jnp.sum(
        grad_sent[targets].reshape(local_rows, 2 * copies, model_width).astype(jnp.float32), axis=1
    )
    gate_term = jnp.sum(grad_gates * gate_values, axis=-1, keepdims=True)
    grad_probs = jnp.sum(chosen * grad_gates[:, :, None], axis=1)
    grad_logits_low = (router_probs * (grad_probs - gate_term)).astype(jnp.bfloat16)
    router_grad = dot_rows(mixed_low, grad_logits_low)
    grad_mixed = dot_last(grad_logits_low, router_weight) + grad_mixed_experts
    unused_two, norm_two_back = jax.vjp(layer_norm, hidden_one, ln2_gain, ln2_shift)
    grad_hidden_part, ln2_gain_grad, ln2_shift_grad = norm_two_back(grad_mixed)
    grad_hidden = grad_out + grad_hidden_part
    grad_attn_low = grad_hidden.astype(jnp.bfloat16)
    grad_attn_all = lax.all_gather(grad_attn_low, "cols", axis=0, tiled=True)
    out_grad = dot_rows(context_low, grad_attn_all)
    grad_context = (
        dot_last(grad_attn_all, out_weight)
        .astype(jnp.bfloat16)
        .reshape(images, SEQ, heads_local, DH)
    )
    scores_again = attention_scores(queries, keys_all, score_scale)
    attn_probs = jnp.exp(scores_again - log_total)
    probs_low = attn_probs.astype(jnp.bfloat16)
    grad_values = jnp.einsum(
        "nhqk,nqhd->nkhd", probs_low, grad_context, preferred_element_type=jnp.float32
    )
    grad_weights = jnp.einsum(
        "nqhd,nkhd->nhqk", grad_context, values_all, preferred_element_type=jnp.float32
    )
    row_term = jnp.sum(grad_weights * attn_probs, axis=-1, keepdims=True)
    grad_scores = (attn_probs * (grad_weights - row_term)).astype(jnp.bfloat16)
    grad_queries = (
        jnp.einsum("nhqk,nkhd->nqhd", grad_scores, keys_all, preferred_element_type=jnp.float32)
        * score_scale
    )
    grad_keys = (
        jnp.einsum("nhqk,nqhd->nkhd", grad_scores, queries, preferred_element_type=jnp.float32)
        * score_scale
    )
    grad_qkv = (
        jnp.stack([grad_queries, grad_keys, grad_values], axis=3)
        .astype(jnp.bfloat16)
        .reshape(pair_rows, 3 * heads_local * DH)
    )
    qkv_grad = dot_rows(gathered, grad_qkv)
    row_block = grad_qkv
    grad_normed = lax.psum_scatter(
        dot_last(row_block, qkv_weight).astype(jnp.bfloat16),
        "cols",
        scatter_dimension=0,
        tiled=True,
    ).astype(jnp.float32)
    unused_one, norm_one_back = jax.vjp(layer_norm, tokens_f, ln1_gain, ln1_shift)
    grad_tokens_part, ln1_gain_grad, ln1_shift_grad = norm_one_back(grad_normed)
    tokens_grad = (grad_hidden + grad_tokens_part).astype(jnp.bfloat16)
    qkv_grad, out_grad = lax.psum((qkv_grad, out_grad), "rows")
    router_grad, ln1_gain_grad, ln1_shift_grad, ln2_gain_grad, ln2_shift_grad = lax.psum(
        (router_grad, ln1_gain_grad, ln1_shift_grad, ln2_gain_grad, ln2_shift_grad),
        ("rows", "cols"),
    )
    return (
        output,
        tokens_grad,
        ln1_gain_grad,
        ln1_shift_grad,
        qkv_grad,
        out_grad,
        ln2_gain_grad,
        ln2_shift_grad,
        router_grad,
        first_grad,
        second_grad,
    )


def solution(mesh):
    in_specs = (
        P(("rows", "cols"), None),
        P(),
        P(),
        P(None, "cols"),
        P("cols", None),
        P(),
        P(),
        P(),
        P(None, ("rows", "cols")),
        P(("rows", "cols"), None),
        P(("rows", "cols"), None),
        P(("rows", "cols"), None),
    )
    out_specs = (
        P(("rows", "cols"), None),
        P(("rows", "cols"), None),
        P(),
        P(),
        P(None, "cols"),
        P("cols", None),
        P(),
        P(),
        P(),
        P(None, ("rows", "cols")),
        P(("rows", "cols"), None),
    )
    return jax.shard_map(body, mesh=mesh, in_specs=in_specs, out_specs=out_specs, check_vma=False)
```

profile of v0, /device:TPU:0, one launch (start us, length us, event | category | flops | bytes accessed | tf_op | source)
XLA Modules:
  0.0 595.0 jit_solution(453533763309978735)
XLA Ops:
  11.4 2.3 all-gather
  14.9 2.8 reshape.405
  17.7 7.0 %fusion.72 = (bf16[2,197,6,1,64]{4,3,2,1,0:T(2,128)(2,1)S(1)}, bf16[2,197,6,1,64]{4,3,2,1,0:T(2,128)(2,1)}, bf16[2,197,6,1,64]{4,3,2,1,0:T(2,128)(2,1)}) fusion(bf16[2,197,6,3,64]{4,3,2,1,0:T(4,128)(2,1)} %reshape.405), kind=kLoop, calls=%fused_computation.161 | loop fusion | bytes 1815552 | tf_op jit(solution)/shard_map/slice | solution.py:78
  24.7 2.5 copy.120
  27.2 3.7 copy.122
  30.9 2.0 copy.121
  39.8 4.9 fusion
  45.4 2.0 collective-permute-start
  50.8 2.1 concatenate
  56.2 3.9 scatter_custom_fusion
  60.0 8.3 %all-to-all-start = ((bf16[16,32,768]{2,1,0:T(8,128)(2,1)}), bf16[16,32,768]{2,1,0:T(8,128)(2,1)}, u32[]{:S(2)}, u32[]{:S(2)}) async-start(bf16[16,32,768]{2,1,0:T(8,128)(2,1)} %bitcast.8), calls=%async_computation | async-start | bytes 1572864 | tf_op jit(solution)/shard_map/all_to_all | solution.py:129
  69.7 2.1 mul.309
  72.2 15.5 %all-to-all-done = bf16[16,32,768]{2,1,0:T(8,128)(2,1)} async-done(((bf16[16,32,768]{2,1,0:T(8,128)(2,1)}), bf16[16,32,768]{2,1,0:T(8,128)(2,1)}, u32[]{:S(2)}, u32[]{:S(2)}) %all-to-all-start) | async-done | bytes 786464 | tf_op jit(solution)/shard_map/all_to_all | solution.py:129
  88.0 3.2 scatter_custom_fusion.1
  91.2 4.9 all-to-all-start.2
  96.2 18.6 %all-to-all-done.2 = bf16[16,32,768]{2,1,0:T(8,128)(2,1)S(1)} async-done(((bf16[16,32,768]{2,1,0:T(8,128)(2,1)}), bf16[16,32,768]{2,1,0:T(8,128)(2,1)S(1)}, u32[]{:S(2)}, u32[]{:S(2)}) %all-to-all-start.2) | async-done | bytes 786464 | tf_op jit(solution)/shard_map/all_to_all | solution.py:136
  115.8 35.3 %fusion.5 = (bf16[1024,3072]{1,0:T(8,128)(2,1)S(1)}, f32[1024,3072]{1,0:T(8,128)}) fusion(s32[3072]{0:T(1024)S(1)} %add_select_fusion, s32[1024]{0:T(1024)S(1)} %add_select_fusion.1, bf16[1024,768]{1,0:T(8,128)(2,1)} %all-gather.5.cloned.1.call-done, bf16[768,3072]{1,0:T(8,128)(2,1)} %param.20), kind=kOutput, calls=%fused_computation.11 | convolution fusion | flops 5042601984 | bytes 25182208 | tf_op jit(solution)/shard_map/dot_general | solution.py:156
  151.1 2.7 copy-done.44
  153.8 8.5 %convolution_convert_fusion.2 = bf16[1024,768]{1,0:T(8,128)(2,1)} fusion(bf16[1024,3072]{1,0:T(8,128)(2,1)S(1)} %get-tuple-element.37, bf16[3072,768]{1,0:T(8,128)(2,1)} %param.21), kind=kOutput, calls=%fused_computation.39 | convolution fusion | flops 4832624640 | bytes 12582912 | tf_op jit(solution)/shard_map/dot_general | solution.py:159
  162.3 8.7 %reduce-scatter.9.cloned.1.call-start = ((), (), s32[]{:S(2)}) async-start(), calls=%async_computation.9 | async-start | bytes 2359296 | tf_op jit(solution)/shard_map/reduce_scatter | solution.py:168
  171.1 12.0 %fusion.2 = bf16[1024,3072]{1,0:T(8,128)(2,1)S(1)} fusion(f32[1024,3072]{1,0:T(8,128)} %get-tuple-element.38, bf16[1024,768]{1,0:T(8,128)(2,1)} %all-gather.7.cloned.1.call-done, bf16[3072,768]{1,0:T(8,128)(2,1)} %param.21, s32[3072]{0:T(1024)S(1)} %add_select_fusion, s32[1024]{0:T(1024)S(1)} %add_select_fusion.1), kind=kOutput, calls=%fused_computation.8 | convolution fusion | flops 4872732672 | bytes 25182208 | tf_op jit(solution)/shard_map/dot_general | solution.py:32
  183.1 2.7 copy-done.43
  185.8 6.3 %convolution_convert_fusion.1 = bf16[1024,768]{1,0:T(8,128)(2,1)} fusion(bf16[1024,3072]{1,0:T(8,128)(2,1)S(1)} %fusion.2, bf16[768,3072]{1,0:T(8,128)(2,1)S(1)} %bitcast.115), kind=kOutput, calls=%fused_computation.38 | convolution fusion | flops 4832624640 | bytes 12582912 | tf_op jit(solution)/shard_map/dot_general | solution.py:32
  192.1 5.2 all-to-all-start.1
  197.2 3.5 reduce-scatter.9.cloned.1.call-done
  200.8 15.2 %all-to-all-done.1 = bf16[16,32,768]{2,1,0:T(8,128)(2,1)S(1)} async-done(((bf16[16,32,768]{2,1,0:T(8,128)(2,1)}), bf16[16,32,768]{2,1,0:T(8,128)(2,1)S(1)}, u32[]{:S(2)}, u32[]{:S(2)}) %all-to-all-start.1) | async-done | bytes 786464 | tf_op jit(solution)/shard_map/all_to_all | solution.py:174
  216.0 4.9 all-to-all-start.3
  220.9 1.8 convert_element_type.105
  222.8 2.6 gather_fusion
  225.4 2.8 reshape.365
  228.2 4.7 multiply_reduce_fusion.2
  234.1 5.3 all-to-all-done.3
  239.5 2.6 gather_fusion.1
  242.1 2.8 reshape.366
  245.0 2.7 reduce_sum.212
  249.8 2.0 fusion.70
  252.8 2.6 all-gather.1
  260.9 3.2 fusion.22
  270.2 4.6 fusion.75
  276.4 10.0 %fusion.79 = f32[3072,768]{1,0:T(8,128)} fusion(bf16[1024,3072]{1,0:T(8,128)(2,1)} %copy-done.44, bf16[1024,768]{1,0:T(8,128)(2,1)} %all-gather.7.cloned.1.call-done), kind=kOutput, calls=%fused_computation.168 | convolution fusion | flops 4831838208 | bytes 17301504 | tf_op jit(solution)/shard_map/dot_general | solution.py:26
  287.7 3.4 fusion.1
  291.8 2.7 collective-permute-start.1
  294.5 9.9 %fusion.78 = f32[768,3072]{1,0:T(8,128)} fusion(bf16[1024,768]{1,0:T(8,128)(2,1)} %all-gather.5.cloned.1.call-done, bf16[1024,3072]{1,0:T(8,128)(2,1)} %copy-done.43), kind=kOutput, calls=%fused_computation.167 | convolution fusion | flops 4831838208 | bytes 17301504 | tf_op jit(solution)/shard_map/dot_general | solution.py:26
  304.4 2.0 concatenate.1
  307.3 40.2 %all-reduce.5 = (f32[768]{0:T(1024)}, f32[768]{0:T(1024)}, f32[768]{0:T(1024)}, f32[768]{0:T(1024)}) all-reduce(f32[768]{0:T(1024)S(1)} %get-tuple-element.15, f32[768]{0:T(1024)S(1)} %get-tuple-element.18, f32[768]{0:T(1024)S(1)} %get-tuple-element.11, ...), channel_id=1, replica_groups=mesh['rows'=16,'cols'=2] {'rows','cols'}, use_global_device_ids=true, to_apply=%region_29.30 | all-reduce | flops 3072 | bytes 24576 | tf_op jit(solution)/shard_map/psum | solution.py:250
  348.6 46.3 %all-reduce.10.cloned.1.call-done = f32[768,32]{0,1:T(8,128)} async-done(((f32[768,32]{0,1:T(8,128)}), f32[768,32]{0,1:T(8,128)}) %all-reduce.10.cloned.1.call-update) | async-done | bytes 98320 | tf_op jit(solution)/shard_map/psum | solution.py:250
  394.8 187.2 %all-reduce.12.cloned.1.call-done = (f32[768,1152]{1,0:T(8,128)}, f32[384,768]{1,0:T(8,128)}) async-done(((f32[768,1152]{1,0:T(8,128)}, f32[384,768]{1,0:T(8,128)}), (f32[768,1152]{1,0:T(8,128)}, f32[384,768]{1,0:T(8,128)})) %all-reduce.12.cloned.1.call-update) | async-done | bytes 4718608 | tf_op jit(solution)/shard_map/psum | solution.py:249
  582.0 4.1 copy.130
  (185 shorter events, 44.7 us)
Async XLA Ops:
  7.2 6.7 %copy-start = (bf16[768,1152]{1,0:T(8,128)(2,1)S(1)}, bf16[768,1152]{1,0:T(8,128)(2,1)}, u32[]{:S(2)}) copy-start(bf16[768,1152]{1,0:T(8,128)(2,1)} %param.15) | copy-start | bytes 5308420
  8.4 3.0 copy-start.29
  27.2 9.4 %copy-start.13 = (bf16[2,197,6,1,64]{1,4,2,0,3:T(8,128)(2,1)}, bf16[2,197,6,1,64]{1,4,2,0,3:T(8,128)(2,1)S(1)}, u32[]{:S(2)}) copy-start(bf16[2,197,6,1,64]{1,4,2,0,3:T(8,128)(2,1)S(1)} %copy.120) | copy-start | bytes 907780
  35.1 12.4 %copy-start.31 = (s32[197,2]{0,1:T(2,128)S(1)}, s32[197,2]{0,1:T(2,128)}, u32[]{:S(2)}) copy-start(s32[197,2]{0,1:T(2,128)} %param.22) | copy-start | bytes 4732
  36.0 13.5 %copy-start.42 = (u32[32]{0:T(128)S(1)}, u32[32]{0:T(128)}, u32[]{:S(2)}) copy-start(u32[32]{0:T(128)} %constant.193) | copy-start | bytes 388
  36.0 16.9 %copy-start.5 = (bf16[197,768]{1,0:T(8,128)(2,1)S(1)}, bf16[197,768]{1,0:T(8,128)(2,1)}, u32[]{:S(2)}) copy-start(bf16[197,768]{1,0:T(8,128)(2,1)} %param.12) | copy-start | bytes 907780
  37.1 16.9 %copy-start.28 = (f32[768]{0:T(1024)S(1)}, f32[768]{0:T(1024)}, u32[]{:S(2)}) copy-start(f32[768]{0:T(1024)} %param.17) | copy-start | bytes 9220
  37.1 16.9 %copy-start.41 = (f32[768]{0:T(1024)S(1)}, f32[768]{0:T(1024)}, u32[]{:S(2)}) copy-start(f32[768]{0:T(1024)} %param.18) | copy-start | bytes 9220
  45.4 5.4 collective-permute-start
  47.9 20.5 %copy-start.9 = (bf16[197,768]{1,0:T(8,128)(2,1)S(1)}, bf16[197,768]{1,0:T(8,128)(2,1)}, u32[]{:S(2)}) copy-start(bf16[197,768]{1,0:T(8,128)(2,1)} %param.23) | copy-start | bytes 907780
  53.4 18.8 %copy-start.39 = (f32[197]{0:T(256)}, f32[197]{0:T(256)S(1)}, u32[]{:S(2)}) copy-start(f32[197]{0:T(256)S(1)} %multiply_reduce_fusion.6) | copy-start | bytes 2368
  53.4 18.5 %copy-start.25 = (bf16[768,32]{0,1:T(8,128)(2,1)S(1)}, bf16[768,32]{0,1:T(8,128)(2,1)}, u32[]{:S(2)}) copy-start(bf16[768,32]{0,1:T(8,128)(2,1)} %param.19) | copy-start | bytes 147460
  53.9 18.2 %copy-start.34 = (f32[197]{0:T(256)}, f32[197]{0:T(256)S(1)}, u32[]{:S(2)}) copy-start(f32[197]{0:T(256)S(1)} %fusion.67) | copy-start | bytes 2368
  54.1 33.6 %copy-start.11 = (bf16[197,768]{1,0:T(8,128)(2,1)}, bf16[197,768]{1,0:T(8,128)(2,1)S(1)}, u32[]{:S(2)}) copy-start(bf16[197,768]{1,0:T(8,128)(2,1)S(1)} %add_convert_fusion.2) | copy-start | bytes 907780
  60.0 27.7 %all-to-all-start = ((bf16[16,32,768]{2,1,0:T(8,128)(2,1)}), bf16[16,32,768]{2,1,0:T(8,128)(2,1)}, u32[]{:S(2)}, u32[]{:S(2)}) async-start(bf16[16,32,768]{2,1,0:T(8,128)(2,1)} %bitcast.8), calls=%async_computation | async-start | bytes 1572864 | tf_op jit(solution)/shard_map/all_to_all | solution.py:129
  68.3 47.4 %all-gather.5.cloned.1.call-start = ((), (), s32[]{:S(2)}) async-start(), calls=%async_computation.6 | async-start | bytes 2359296 | tf_op jit(solution)/shard_map/all_gather | solution.py:148
  72.2 15.5 %copy-start.36 = (f32[197]{0:T(256)}, f32[197]{0:T(256)S(1)}, u32[]{:S(2)}) copy-start(f32[197]{0:T(256)S(1)} %fusion.55) | copy-start | bytes 2368
  91.2 23.5 %all-to-all-start.2 = ((bf16[16,32,768]{2,1,0:T(8,128)(2,1)}), bf16[16,32,768]{2,1,0:T(8,128)(2,1)S(1)}, u32[]{:S(2)}, u32[]{:S(2)}) async-start(bf16[16,32,768]{2,1,0:T(8,128)(2,1)} %bitcast.107), calls=%async_computation.3 | async-start | bytes 1572864 | tf_op jit(solution)/shard_map/all_to_all | solution.py:136
  96.1 74.9 %all-gather.7.cloned.1.call-start = ((), (), s32[]{:S(2)}) async-start(), calls=%async_computation.8 | async-start | bytes 2359296 | tf_op jit(solution)/shard_map/all_gather | solution.py:149
  115.7 76.4 %reduce-scatter.7.cloned.1.call-start = ((), (), s32[]{:S(2)}) async-start(), calls=%async_computation.7 | async-start | bytes 2359296 | tf_op jit(solution)/shard_map/reduce_scatter | solution.py:158
  151.0 2.7 copy-start.44
  153.8 32.0 %slice-start = ((s8[4718592]{0:T(1024)(128)(4,1)}), s8[524288]{0:T(1024)(128)(4,1)S(1)}, s32[]{:S(2)}) async-start(s8[4718592]{0:T(1024)(128)(4,1)} %bitcast.114), calls=%async_computation.12 | async-start | bytes 1048576
  162.3 38.5 %reduce-scatter.9.cloned.1.call-start = ((), (), s32[]{:S(2)}) async-start(), calls=%async_computation.9 | async-start | bytes 2359296 | tf_op jit(solution)/shard_map/reduce_scatter | solution.py:168
  171.1 14.7 %slice-start.1 = ((s8[4718592]{0:T(1024)(128)(4,1)}), s8[4194304]{0:T(1024)(128)(4,1)S(1)}, s32[]{:S(2)}) async-start(s8[4718592]{0:T(1024)(128)(4,1)} %bitcast.114), calls=%async_computation.13 | async-start | bytes 8388608
  183.1 2.7 copy-start.43
  192.1 23.9 %all-to-all-start.1 = ((bf16[16,32,768]{2,1,0:T(8,128)(2,1)}), bf16[16,32,768]{2,1,0:T(8,128)(2,1)S(1)}, u32[]{:S(2)}, u32[]{:S(2)}) async-start(bf16[16,32,768]{2,1,0:T(8,128)(2,1)} %bitcast.109), calls=%async_computation.2 | async-start | bytes 1572864 | tf_op jit(solution)/shard_map/all_to_all | solution.py:174
  216.0 23.5 %all-to-all-start.3 = ((bf16[16,32,768]{2,1,0:T(8,128)(2,1)}), bf16[16,32,768]{2,1,0:T(8,128)(2,1)S(1)}, u32[]{:S(2)}, u32[]{:S(2)}) async-start(bf16[16,32,768]{2,1,0:T(8,128)(2,1)} %bitcast.108), calls=%async_computation.5 | async-start | bytes 1572864 | tf_op jit(solution)/shard_map/all_to_all | solution.py:187
  220.9 174.0 %all-reduce.10.cloned.1.call-start = ((), (), s32[]{:S(2)}) async-start(), calls=%async_computation.10 | async-start | bytes 196608 | tf_op jit(solution)/shard_map/psum | solution.py:250
  232.8 15.6 %copy-start.4 = (f32[197,768]{1,0:T(8,128)S(1)}, f32[197,768]{1,0:T(8,128)}, u32[]{:S(2)}) copy-start(f32[197,768]{1,0:T(8,128)} %copy-done.3) | copy-start | bytes 1815556
  242.1 7.6 %copy-start.40 = (f32[197]{0:T(256)S(1)}, f32[197]{0:T(256)}, u32[]{:S(2)}) copy-start(f32[197]{0:T(256)} %copy-done.39) | copy-start | bytes 2368
  242.1 7.7 %copy-start.35 = (f32[197]{0:T(256)S(1)}, f32[197]{0:T(256)}, u32[]{:S(2)}) copy-start(f32[197]{0:T(256)} %copy-done.34) | copy-start | bytes 2368
  242.1 10.5 %copy-start.10 = (bf16[197,768]{1,0:T(8,128)(2,1)S(1)}, bf16[197,768]{1,0:T(8,128)(2,1)}, u32[]{:S(2)}) copy-start(bf16[197,768]{1,0:T(8,128)(2,1)} %param.23) | copy-start | bytes 907780
  252.8 11.3 %copy-start.14 = (bf16[2,197,6,1,64]{1,4,2,0,3:T(8,128)(2,1)S(1)}, bf16[2,197,6,1,64]{1,4,2,0,3:T(8,128)(2,1)}, u32[]{:S(2)}) copy-start(bf16[2,197,6,1,64]{1,4,2,0,3:T(8,128)(2,1)} %copy-done.13) | copy-start | bytes 907780
  260.9 3.2 copy-start.2
  264.9 2.3 copy-start.20
  270.2 4.7 copy-start.17
  270.2 4.7 copy-start.19
  274.9 307.1 %all-reduce.12.cloned.1.call-start = ((), (), s32[]{:S(2)}) async-start(), calls=%async_computation.11 | async-start | bytes 9437184 | tf_op jit(solution)/shard_map/psum | solution.py:249
  276.4 10.0 %copy-start.23 = (bf16[394,1152]{0,1:T(8,128)(2,1)S(1)}, bf16[394,1152]{0,1:T(8,128)(2,1)}, u32[]{:S(2)}) copy-start(bf16[394,1152]{0,1:T(8,128)(2,1)} %convert_element_type.115) | copy-start | bytes 2723332
  291.8 14.7 %copy-start.6 = (bf16[197,768]{1,0:T(8,128)(2,1)S(1)}, bf16[197,768]{1,0:T(8,128)(2,1)}, u32[]{:S(2)}) copy-start(bf16[197,768]{1,0:T(8,128)(2,1)} %param.12) | copy-start | bytes 907780
  291.8 14.7 %copy-start.27 = (f32[768]{0:T(1024)S(1)}, f32[768]{0:T(1024)}, u32[]{:S(2)}) copy-start(f32[768]{0:T(1024)} %param.13) | copy-start | bytes 9220
  291.8 14.7 %copy-start.30 = (f32[197]{0:T(256)S(1)}, f32[197]{0:T(256)}, u32[]{:S(2)}) copy-start(f32[197]{0:T(256)} %copy-done.29) | copy-start | bytes 2368
  291.8 15.0 %copy-start.38 = (f32[197]{0:T(256)S(1)}, f32[197]{0:T(256)}, u32[]{:S(2)}) copy-start(f32[197]{0:T(256)} %copy-done.37) | copy-start | bytes 2368
  291.8 15.0 %copy-start.33 = (f32[197]{0:T(256)S(1)}, f32[197]{0:T(256)}, u32[]{:S(2)}) copy-start(f32[197]{0:T(256)} %copy-done.32) | copy-start | bytes 2368
  291.8 55.6 %copy-start.8 = (f32[197,768]{1,0:T(8,128)S(1)}, f32[197,768]{1,0:T(8,128)}, u32[]{:S(2)}) copy-start(f32[197,768]{1,0:T(8,128)} %copy-done.7) | copy-start | bytes 1815556
  291.8 12.5 %collective-permute-start.1 = (bf16[3,768]{1,0:T(4,128)(2,1)S(1)}, bf16[3,768]{1,0:T(4,128)(2,1)S(1)}, u32[]{:S(2)}, u32[]{:S(2)}) collective-permute-start(bf16[3,768]{1,0:T(4,128)(2,1)S(1)} %slice.34), channel_id=1, source_target_pairs={{0,1},{2,3},{4,5},{6,7},{8,9},{10,11},{12,13},{14,15},{16,17},{18,... | collective-permute-start | bytes 13832
  582.0 4.1 copy-start.22
  582.0 5.1 copy-start.26
  (11 other events, 11.5 us)
Sparse Core Ops, SparseCore 0:
  87.9 9.0 all-gather.4
  115.8 9.0 all-gather.6
  162.4 8.3 reduce-scatter.6
  192.2 8.5 reduce-scatter.8
  275.0 119.7 all-reduce.9
  401.0 180.9 all-reduce.11
where the time goes:
time: 605 us; the launch traced here: 595 us
  waiting for transfers between devices  292 us (48%)
  matrix products  103 us (17%)
  local copies, waits for them, and re-layouts  68.5 us (11%)
  blocking collectives  53.4 us (9%)
  starting transfers between devices  36.9 us (6%)
  other arithmetic  25.5 us (4%)
  between operations  16.1 us (3%)
    psum x1, waiting for transfers between devices, body(): qkv_grad, out_grad = lax.psum((qkv_grad, out_grad), 'rows')  187 us
    psum x1, waiting for transfers between devices, body(): lax.psum((router_grad, ln1_gain_grad, ln1_shift_grad, ln2_gain_grad, ln2_...  46.3 us
    psum x1, blocking collectives, body(): lax.psum((router_grad, ln1_gain_grad, ln1_shift_grad, ln2_gain_grad, ln2_...  40.2 us
    dot_general x1, matrix products, body(): jnp.dot(both_rows, expert_in, preferred_element_type=jnp.float32) * mask  35.3 us
    unnamed x108, local copies, waits for them, and re-layouts  30.5 us
    dot_general x5, matrix products, dot_rows(): lax.dot_general(first_side, second_side, (((0,), (0,)), ((), ())), prefer...  26.8 us
    dot_general x5, matrix products, dot_last(): lax.dot_general(first_side, second_side, (((1,), (1,)), ((), ())), prefer...  22.5 us
    all_to_all x1, waiting for transfers between devices, body(): lax.all_to_all(grads_send.reshape(row_count, slots, model_width), 'rows',...  18.6 us
  transfers between devices with their start and end apart: 12, of which 7 were waited for; matrix products, arithmetic and copies ran while one was open for 19% of the time, Pallas kernels for 0%

commit v1 on v0

--- a/solution.py
+++ b/solution.py
@@ -53,6 +53,29 @@
     routes,
     cotangent,
 ):
+
+    def _compute_tails(work_x):
+        high = jax.lax.axis_index("rows")
+        formed = jax.lax.axis_size("rows")
+        back, opened = (formed, high)
+        val = work_x.shape[0] // back
+        h_now = list(work_x.shape)
+        h_now[0] = val
+        field_out = h_now[0]
+        h_now[0] = field_out * back
+        new = jnp.zeros(h_now, work_x.dtype)
+        for idx in range(back):
+            local_part = lax.dynamic_slice_in_dim(work_x, (opened ^ idx) * val, val, axis=0)
+            if idx:
+                nodes = []
+                for pp in range(back):
+                    nodes.append((pp, pp ^ idx))
+                local_part = jax.lax.ppermute(local_part, "rows", nodes)
+            new = lax.dynamic_update_slice_in_dim(
+                new, local_part, (opened ^ idx) * field_out, axis=0
+            )
+        return new
+
     local_rows = tokens_in.shape[0]
     model_width = tokens_in.shape[1]
     experts = router_weight.shape[1]
@@ -126,13 +149,7 @@
         .set(jnp.repeat(grad_slots, copies, axis=0))
     )
     arrived, grad_result = (
-        lax.all_to_all(
-            rows_send.reshape(row_count, slots, model_width),
-            "rows",
-            split_axis=0,
-            concat_axis=0,
-            tiled=True,
-        ),
+        _compute_tails(rows_send.reshape(row_count, slots, model_width)),
         lax.all_to_all(
             grads_send.reshape(row_count, slots, model_width),
             "rows",

time: 605 us -> 578 us (0.955)
  waiting for transfers between devices: 292 us -> 240 us
  local copies, waits for them, and re-layouts: 68.5 us -> 84.5 us
  starting transfers between devices: 36.9 us -> 46 us
    psum x1, waiting for transfers between devices: 46.3 us -> 9.37 us  [body(): lax.psum((router_grad, ln1_gain_grad, ln1_shift_grad, ln2_gain_grad, ln2_...]
    ppermute x0 -> x15, starting transfers between devices: none -> 27.7 us  [_compute_tails(): local_part = jax.lax.ppermute(local_part, 'rows', nodes)]
    all_to_all x1 -> x0, waiting for transfers between devices: 15.5 us -> none  [body(): lax.all_to_all(rows_send.reshape(row_count, slots, model_width), 'rows',...]
    dynamic_update_slice x0 -> x15, local copies, waits for them, and re-layouts: none -> 9.35 us  [_compute_tails(): lax.dynamic_update_slice_in_dim(new, local_part, (opened ^ idx) * field_o...]
    reduce_scatter x1, starting transfers between devices: 8.75 us -> 0.45 us  [body(): lax.psum_scatter(dot_last(grad_pre_low, expert_in).astype(jnp.bfloat16),...]
    all_to_all x1 -> x0, starting transfers between devices: 8.28 us -> none  [body(): lax.all_to_all(rows_send.reshape(row_count, slots, model_width), 'rows',...]
    unnamed x108 -> x98, local copies, waits for them, and re-layouts: 30.5 us -> 31.9 us
  transfers between devices with their start and end apart: 12 -> 26, of which waited for: 7 -> 7; matrix products, arithmetic and copies ran while one was open for 19% -> 27% of each run, Pallas kernels for 0% -> 0%
where the time goes in v1:
time: 578 us; the launch traced here: 571 us
  waiting for transfers between devices  240 us (42%)
  matrix products  104 us (18%)
  local copies, waits for them, and re-layouts  84.5 us (15%)
  blocking collectives  53.1 us (9%)
  starting transfers between devices  46 us (8%)
  other arithmetic  27.9 us (5%)
  between operations  16 us (3%)
    psum x1, waiting for transfers between devices, body(): qkv_grad, out_grad = lax.psum((qkv_grad, out_grad), 'rows')  187 us
    psum x1, blocking collectives, body(): lax.psum((router_grad, ln1_gain_grad, ln1_shift_grad, ln2_gain_grad, ln2_...  39.6 us
    dot_general x1, matrix products, body(): jnp.dot(both_rows, expert_in, preferred_element_type=jnp.float32) * mask  35.3 us
    unnamed x98, local copies, waits for them, and re-layouts  31.9 us
    ppermute x15, starting transfers between devices, _compute_tails(): local_part = jax.lax.ppermute(local_part, 'rows', nodes)  27.7 us
    dot_general x5, matrix products, dot_rows(): lax.dot_general(first_side, second_side, (((0,), (0,)), ((), ())), prefer...  26.8 us
    dot_general x5, matrix products, dot_last(): lax.dot_general(first_side, second_side, (((1,), (1,)), ((), ())), prefer...  22.9 us
    all_to_all x1, waiting for transfers between devices, body(): lax.all_to_all(grads_send.reshape(row_count, slots, model_width), 'rows',...  15.1 us
  transfers between devices with their start and end apart: 26, of which 7 were waited for; matrix products, arithmetic and copies ran while one was open for 27% of the time, Pallas kernels for 0%

profile of v1, /device:TPU:0, one launch (start us, length us, event | category | flops | bytes accessed | tf_op | source)
XLA Modules:
  0.0 571.0 jit_solution(5984266279915376749)
XLA Ops:
  11.5 2.3 all-gather
  15.0 2.8 reshape.405
  17.8 7.0 %fusion.72 = (bf16[2,197,6,1,64]{4,3,2,1,0:T(2,128)(2,1)S(1)}, bf16[2,197,6,1,64]{4,3,2,1,0:T(2,128)(2,1)}, bf16[2,197,6,1,64]{4,3,2,1,0:T(2,128)(2,1)}) fusion(bf16[2,197,6,3,64]{4,3,2,1,0:T(4,128)(2,1)} %reshape.405), kind=kLoop, calls=%fused_computation.192 | loop fusion | bytes 1815552 | tf_op jit(solution)/shard_map/slice | solution.py:101
  24.8 2.5 copy.120
  27.3 3.7 copy.122
  39.1 2.8 fusion.74
  41.9 5.2 fusion
  58.7 3.5 concatenate
  66.3 2.6 reshape.387
  68.9 3.6 scatter_custom_fusion
  75.3 2.9 collective-permute-start
  83.4 2.6 collective-permute-start.5
  87.3 2.9 collective-permute-start.7
  92.8 3.5 collective-permute-start.9
  97.6 3.9 collective-permute-start.11
  103.8 4.6 collective-permute-start.13
  112.1 4.5 collective-permute-done.14
  117.6 3.2 scatter_custom_fusion.1
  120.8 3.6 all-to-all-start.1
  124.5 15.1 %all-to-all-done.1 = bf16[16,32,768]{2,1,0:T(8,128)(2,1)S(1)} async-done(((bf16[16,32,768]{2,1,0:T(8,128)(2,1)}), bf16[16,32,768]{2,1,0:T(8,128)(2,1)S(1)}, u32[]{:S(2)}, u32[]{:S(2)}) %all-to-all-start.1) | async-done | bytes 786464 | tf_op jit(solution)/shard_map/all_to_all | solution.py:153
  140.9 35.3 %fusion.5 = (bf16[1024,3072]{1,0:T(8,128)(2,1)S(1)}, f32[1024,3072]{1,0:T(8,128)}) fusion(s32[3072]{0:T(1024)S(1)} %add_select_fusion, s32[1024]{0:T(1024)S(1)} %add_select_fusion.1, bf16[1024,768]{1,0:T(8,128)(2,1)} %all-gather.5.cloned.1.call-done, bf16[768,3072]{1,0:T(8,128)(2,1)} %param.20), kind=kOutput, calls=%fused_computation.11 | convolution fusion | flops 5042601984 | bytes 25182208 | tf_op jit(solution)/shard_map/dot_general | solution.py:173
  176.2 2.7 copy-done.39
  178.9 8.5 %convolution_convert_fusion.2 = bf16[1024,768]{1,0:T(8,128)(2,1)} fusion(bf16[1024,3072]{1,0:T(8,128)(2,1)S(1)} %get-tuple-element.53, bf16[3072,768]{1,0:T(8,128)(2,1)} %param.21), kind=kOutput, calls=%fused_computation.39 | convolution fusion | flops 4832624640 | bytes 12582912 | tf_op jit(solution)/shard_map/dot_general | solution.py:176
  187.9 12.1 %fusion.2 = bf16[1024,3072]{1,0:T(8,128)(2,1)S(1)} fusion(f32[1024,3072]{1,0:T(8,128)} %get-tuple-element.54, bf16[1024,768]{1,0:T(8,128)(2,1)} %all-gather.7.cloned.1.call-done, bf16[3072,768]{1,0:T(8,128)(2,1)} %param.21, s32[3072]{0:T(1024)S(1)} %add_select_fusion, s32[1024]{0:T(1024)S(1)} %add_select_fusion.1), kind=kOutput, calls=%fused_computation.8 | convolution fusion | flops 4872732672 | bytes 25182208 | tf_op jit(solution)/shard_map/dot_general | solution.py:32
  200.0 2.7 copy-done.38
  202.7 6.3 %convolution_convert_fusion.1 = bf16[1024,768]{1,0:T(8,128)(2,1)} fusion(bf16[1024,3072]{1,0:T(8,128)(2,1)S(1)} %fusion.2, bf16[768,3072]{1,0:T(8,128)(2,1)S(1)} %bitcast.116), kind=kOutput, calls=%fused_computation.38 | convolution fusion | flops 4832624640 | bytes 12582912 | tf_op jit(solution)/shard_map/dot_general | solution.py:32
  209.0 4.6 all-to-all-start
  213.6 3.5 reduce-scatter.9.cloned.1.call-done
  217.1 14.4 %all-to-all-done = bf16[16,32,768]{2,1,0:T(8,128)(2,1)S(1)} async-done(((bf16[16,32,768]{2,1,0:T(8,128)(2,1)}), bf16[16,32,768]{2,1,0:T(8,128)(2,1)S(1)}, u32[]{:S(2)}, u32[]{:S(2)}) %all-to-all-start) | async-done | bytes 786464 | tf_op jit(solution)/shard_map/all_to_all | solution.py:191
  231.5 4.4 all-to-all-start.2
  237.8 2.6 gather_fusion
  240.4 2.8 reshape.365
  243.3 4.7 multiply_reduce_fusion.2
  249.0 5.5 all-to-all-done.2
  254.4 2.6 gather_fusion.1
  257.1 2.8 reshape.366
  259.9 3.5 reduce_sum.212
  268.0 2.6 all-gather.1
  276.1 2.4 fusion.22
  283.9 4.6 fusion.75
  290.0 10.0 %fusion.79 = f32[3072,768]{1,0:T(8,128)} fusion(bf16[1024,3072]{1,0:T(8,128)(2,1)} %copy-done.39, bf16[1024,768]{1,0:T(8,128)(2,1)} %all-gather.7.cloned.1.call-done), kind=kOutput, calls=%fused_computation.199 | convolution fusion | flops 4831838208 | bytes 17301504 | tf_op jit(solution)/shard_map/dot_general | solution.py:26
  301.3 3.4 fusion.1
  305.5 2.6 collective-permute-start.16
  308.1 9.9 %fusion.78 = f32[768,3072]{1,0:T(8,128)} fusion(bf16[1024,768]{1,0:T(8,128)(2,1)} %all-gather.5.cloned.1.call-done, bf16[1024,3072]{1,0:T(8,128)(2,1)} %copy-done.38), kind=kOutput, calls=%fused_computation.198 | convolution fusion | flops 4831838208 | bytes 17301504 | tf_op jit(solution)/shard_map/dot_general | solution.py:26
  320.8 39.6 %all-reduce.5 = (f32[768]{0:T(1024)}, f32[768]{0:T(1024)}, f32[768]{0:T(1024)}, f32[768]{0:T(1024)}) all-reduce(f32[768]{0:T(1024)S(1)} %get-tuple-element.15, f32[768]{0:T(1024)S(1)} %get-tuple-element.18, f32[768]{0:T(1024)S(1)} %get-tuple-element.11, ...), channel_id=1, replica_groups=mesh['rows'=16,'cols'=2] {'rows','cols'}, use_global_device_ids=true, to_apply=%region_29.30 | all-reduce | flops 3072 | bytes 24576 | tf_op jit(solution)/shard_map/psum | solution.py:267
  361.6 9.4 %all-reduce.10.cloned.1.call-done = f32[768,32]{0,1:T(8,128)} async-done(((f32[768,32]{0,1:T(8,128)}), f32[768,32]{0,1:T(8,128)}) %all-reduce.10.cloned.1.call-update) | async-done | bytes 98320 | tf_op jit(solution)/shard_map/psum | solution.py:267
  370.9 187.2 %all-reduce.12.cloned.1.call-done = (f32[768,1152]{1,0:T(8,128)}, f32[384,768]{1,0:T(8,128)}) async-done(((f32[768,1152]{1,0:T(8,128)}, f32[384,768]{1,0:T(8,128)}), (f32[768,1152]{1,0:T(8,128)}, f32[384,768]{1,0:T(8,128)})) %all-reduce.12.cloned.1.call-update) | async-done | bytes 4718608 | tf_op jit(solution)/shard_map/psum | solution.py:266
  558.1 4.1 copy.146
  (220 shorter events, 77.4 us)
Async XLA Ops:
  7.2 133.7 %all-gather.5.cloned.1.call-start = ((), (), s32[]{:S(2)}) async-start(), calls=%async_computation.5 | async-start | bytes 2359296 | tf_op jit(solution)/shard_map/all_gather | solution.py:165
  27.3 9.4 %copy-start.13 = (bf16[2,197,6,1,64]{1,4,2,0,3:T(8,128)(2,1)}, bf16[2,197,6,1,64]{1,4,2,0,3:T(8,128)(2,1)S(1)}, u32[]{:S(2)}) copy-start(bf16[2,197,6,1,64]{1,4,2,0,3:T(8,128)(2,1)S(1)} %copy.120) | copy-start | bytes 907780
  35.1 14.2 %copy-start.33 = (s32[197,2]{0,1:T(2,128)S(1)}, s32[197,2]{0,1:T(2,128)}, u32[]{:S(2)}) copy-start(s32[197,2]{0,1:T(2,128)} %param.22) | copy-start | bytes 4732
  36.1 19.0 %copy-start.9 = (bf16[197,768]{1,0:T(8,128)(2,1)S(1)}, bf16[197,768]{1,0:T(8,128)(2,1)}, u32[]{:S(2)}) copy-start(bf16[197,768]{1,0:T(8,128)(2,1)} %param.23) | copy-start | bytes 907780
  39.1 16.0 %copy-start.17 = (bf16[394,384]{0,1:T(8,128)(2,1)}, bf16[394,384]{0,1:T(8,128)(2,1)S(1)}, u32[]{:S(2)}) copy-start(bf16[394,384]{0,1:T(8,128)(2,1)S(1)} %reshape.350) | copy-start | bytes 907780
  39.1 23.1 %copy-start.5 = (bf16[197,768]{1,0:T(8,128)(2,1)S(1)}, bf16[197,768]{1,0:T(8,128)(2,1)}, u32[]{:S(2)}) copy-start(bf16[197,768]{1,0:T(8,128)(2,1)} %param.12) | copy-start | bytes 907780
  41.9 22.4 %copy-start.30 = (f32[768]{0:T(1024)S(1)}, f32[768]{0:T(1024)}, u32[]{:S(2)}) copy-start(f32[768]{0:T(1024)} %param.17) | copy-start | bytes 9220
  47.1 8.0 %copy-start.20 = (f32[200,768]{1,0:T(8,128)}, f32[200,768]{1,0:T(8,128)S(1)}, u32[]{:S(2)}) copy-start(f32[200,768]{1,0:T(8,128)S(1)} %fusion) | copy-start | bytes 1843204
  47.1 11.6 %collective-permute-start.15 = (f32[3,768]{1,0:T(4,128)S(1)}, f32[3,768]{1,0:T(4,128)S(1)}, u32[]{:S(2)}, u32[]{:S(2)}) collective-permute-start(f32[3,768]{1,0:T(4,128)S(1)} %slice.33), channel_id=1, source_target_pairs={{0,1},{2,3},{4,5},{6,7},{8,9},{10,11},{12,13},{14,15},{16,17},{18,... | collective-permute-start | bytes 27656
  58.7 24.4 %copy-start.26 = (bf16[768,32]{0,1:T(8,128)(2,1)S(1)}, bf16[768,32]{0,1:T(8,128)(2,1)}, u32[]{:S(2)}) copy-start(bf16[768,32]{0,1:T(8,128)(2,1)} %param.19) | copy-start | bytes 147460
  65.1 55.7 %copy-start.11 = (bf16[197,768]{1,0:T(8,128)(2,1)}, bf16[197,768]{1,0:T(8,128)(2,1)S(1)}, u32[]{:S(2)}) copy-start(bf16[197,768]{1,0:T(8,128)(2,1)S(1)} %add_convert_fusion.2) | copy-start | bytes 907780
  75.3 8.1 %collective-permute-start = (bf16[1,32,768]{2,1,0:T(8,128)(2,1)S(1)}, bf16[1,32,768]{2,1,0:T(8,128)(2,1)S(1)}, u32[]{:S(2)}, u32[]{:S(2)}) collective-permute-start(bf16[1,32,768]{2,1,0:T(8,128)(2,1)S(1)} %get-tuple-element.46), channel_id=1, source_target_pairs={{0,2},{2,0},{4,6},{6,4},{8,10},{10,8},{12,14},{14,12},{16,18},{18,... | collective-permute-start | bytes 147464 | tf_op jit(solution)/shard_map/ppermute | solution.py:73
  78.2 8.5 %collective-permute-start.1 = (bf16[1,32,768]{2,1,0:T(8,128)(2,1)S(1)}, bf16[1,32,768]{2,1,0:T(8,128)(2,1)S(1)}, u32[]{:S(2)}, u32[]{:S(2)}) collective-permute-start(bf16[1,32,768]{2,1,0:T(8,128)(2,1)S(1)} %get-tuple-element.45), channel_id=1, source_target_pairs={{0,4},{2,6},{4,0},{6,2},{8,12},{10,14},{12,8},{14,10},{16,20},{18,... | collective-permute-start | bytes 147464 | tf_op jit(solution)/shard_map/ppermute | solution.py:73
  79.7 7.6 %collective-permute-start.2 = (bf16[1,32,768]{2,1,0:T(8,128)(2,1)S(1)}, bf16[1,32,768]{2,1,0:T(8,128)(2,1)S(1)}, u32[]{:S(2)}, u32[]{:S(2)}) collective-permute-start(bf16[1,32,768]{2,1,0:T(8,128)(2,1)S(1)} %get-tuple-element.44), channel_id=1, source_target_pairs={{0,6},{2,4},{4,2},{6,0},{8,14},{10,12},{12,10},{14,8},{16,22},{18,... | collective-permute-start | bytes 147464 | tf_op jit(solution)/shard_map/ppermute | solution.py:73
  79.7 11.2 %collective-permute-start.3 = (bf16[1,32,768]{2,1,0:T(8,128)(2,1)S(1)}, bf16[1,32,768]{2,1,0:T(8,128)(2,1)S(1)}, u32[]{:S(2)}, u32[]{:S(2)}) collective-permute-start(bf16[1,32,768]{2,1,0:T(8,128)(2,1)S(1)} %get-tuple-element.43), channel_id=1, source_target_pairs={{0,8},{2,10},{4,12},{6,14},{8,0},{10,2},{12,4},{14,6},{16,24},{18,... | collective-permute-start | bytes 147464 | tf_op jit(solution)/shard_map/ppermute | solution.py:73
  81.7 11.0 %collective-permute-start.4 = (bf16[1,32,768]{2,1,0:T(8,128)(2,1)S(1)}, bf16[1,32,768]{2,1,0:T(8,128)(2,1)S(1)}, u32[]{:S(2)}, u32[]{:S(2)}) collective-permute-start(bf16[1,32,768]{2,1,0:T(8,128)(2,1)S(1)} %get-tuple-element.42), channel_id=1, source_target_pairs={{0,10},{2,8},{4,14},{6,12},{8,2},{10,0},{12,6},{14,4},{16,26},{18,... | collective-permute-start | bytes 147464 | tf_op jit(solution)/shard_map/ppermute | solution.py:73
  83.4 13.5 %collective-permute-start.5 = (bf16[1,32,768]{2,1,0:T(8,128)(2,1)S(1)}, bf16[1,32,768]{2,1,0:T(8,128)(2,1)S(1)}, u32[]{:S(2)}, u32[]{:S(2)}) collective-permute-start(bf16[1,32,768]{2,1,0:T(8,128)(2,1)S(1)} %get-tuple-element.41), channel_id=1, source_target_pairs={{0,12},{2,14},{4,8},{6,10},{8,4},{10,6},{12,0},{14,2},{16,28},{18,... | collective-permute-start | bytes 147464 | tf_op jit(solution)/shard_map/ppermute | solution.py:73
  86.7 10.9 %collective-permute-start.6 = (bf16[1,32,768]{2,1,0:T(8,128)(2,1)S(1)}, bf16[1,32,768]{2,1,0:T(8,128)(2,1)S(1)}, u32[]{:S(2)}, u32[]{:S(2)}) collective-permute-start(bf16[1,32,768]{2,1,0:T(8,128)(2,1)S(1)} %get-tuple-element.40), channel_id=1, source_target_pairs={{0,14},{2,12},{4,10},{6,8},{8,6},{10,4},{12,2},{14,0},{16,30},{18,... | collective-permute-start | bytes 147464 | tf_op jit(solution)/shard_map/ppermute | solution.py:73
  87.3 14.7 %collective-permute-start.7 = (bf16[1,32,768]{2,1,0:T(8,128)(2,1)S(1)}, bf16[1,32,768]{2,1,0:T(8,128)(2,1)S(1)}, u32[]{:S(2)}, u32[]{:S(2)}) collective-permute-start(bf16[1,32,768]{2,1,0:T(8,128)(2,1)S(1)} %get-tuple-element.39), channel_id=1, source_target_pairs={{0,16},{2,18},{4,20},{6,22},{8,24},{10,26},{12,28},{14,30},{16,0},... | collective-permute-start | bytes 147464 | tf_op jit(solution)/shard_map/ppermute | solution.py:73
  90.9 12.9 %collective-permute-start.8 = (bf16[1,32,768]{2,1,0:T(8,128)(2,1)S(1)}, bf16[1,32,768]{2,1,0:T(8,128)(2,1)S(1)}, u32[]{:S(2)}, u32[]{:S(2)}) collective-permute-start(bf16[1,32,768]{2,1,0:T(8,128)(2,1)S(1)} %get-tuple-element.38), channel_id=1, source_target_pairs={{0,18},{2,16},{4,22},{6,20},{8,26},{10,24},{12,30},{14,28},{16,2},... | collective-permute-start | bytes 147464 | tf_op jit(solution)/shard_map/ppermute | solution.py:73
  92.8 16.2 %collective-permute-start.9 = (bf16[1,32,768]{2,1,0:T(8,128)(2,1)S(1)}, bf16[1,32,768]{2,1,0:T(8,128)(2,1)S(1)}, u32[]{:S(2)}, u32[]{:S(2)}) collective-permute-start(bf16[1,32,768]{2,1,0:T(8,128)(2,1)S(1)} %get-tuple-element.37), channel_id=1, source_target_pairs={{0,20},{2,22},{4,16},{6,18},{8,28},{10,30},{12,24},{14,26},{16,4},... | collective-permute-start | bytes 147464 | tf_op jit(solution)/shard_map/ppermute | solution.py:73
  96.9 12.7 %collective-permute-start.10 = (bf16[1,32,768]{2,1,0:T(8,128)(2,1)S(1)}, bf16[1,32,768]{2,1,0:T(8,128)(2,1)S(1)}, u32[]{:S(2)}, u32[]{:S(2)}) collective-permute-start(bf16[1,32,768]{2,1,0:T(8,128)(2,1)S(1)} %get-tuple-element.36), channel_id=1, source_target_pairs={{0,22},{2,20},{4,18},{6,16},{8,30},{10,28},{12,26},{14,24},{16,6},... | collective-permute-start | bytes 147464 | tf_op jit(solution)/shard_map/ppermute | solution.py:73
  97.6 12.7 %collective-permute-start.11 = (bf16[1,32,768]{2,1,0:T(8,128)(2,1)S(1)}, bf16[1,32,768]{2,1,0:T(8,128)(2,1)S(1)}, u32[]{:S(2)}, u32[]{:S(2)}) collective-permute-start(bf16[1,32,768]{2,1,0:T(8,128)(2,1)S(1)} %get-tuple-element.35), channel_id=1, source_target_pairs={{0,24},{2,26},{4,28},{6,30},{8,16},{10,18},{12,20},{14,22},{16,8},... | collective-permute-start | bytes 147464 | tf_op jit(solution)/shard_map/ppermute | solution.py:73
  102.0 8.9 %collective-permute-start.12 = (bf16[1,32,768]{2,1,0:T(8,128)(2,1)S(1)}, bf16[1,32,768]{2,1,0:T(8,128)(2,1)S(1)}, u32[]{:S(2)}, u32[]{:S(2)}) collective-permute-start(bf16[1,32,768]{2,1,0:T(8,128)(2,1)S(1)} %get-tuple-element.34), channel_id=1, source_target_pairs={{0,26},{2,24},{4,30},{6,28},{8,18},{10,16},{12,22},{14,20},{16,10}... | collective-permute-start | bytes 147464 | tf_op jit(solution)/shard_map/ppermute | solution.py:73
  103.8 7.7 %collective-permute-start.13 = (bf16[1,32,768]{2,1,0:T(8,128)(2,1)S(1)}, bf16[1,32,768]{2,1,0:T(8,128)(2,1)S(1)}, u32[]{:S(2)}, u32[]{:S(2)}) collective-permute-start(bf16[1,32,768]{2,1,0:T(8,128)(2,1)S(1)} %get-tuple-element.33), channel_id=1, source_target_pairs={{0,28},{2,30},{4,24},{6,26},{8,20},{10,22},{12,16},{14,18},{16,12}... | collective-permute-start | bytes 147464 | tf_op jit(solution)/shard_map/ppermute | solution.py:73
  109.0 7.7 %collective-permute-start.14 = (bf16[1,32,768]{2,1,0:T(8,128)(2,1)S(1)}, bf16[1,32,768]{2,1,0:T(8,128)(2,1)S(1)}, u32[]{:S(2)}, u32[]{:S(2)}) collective-permute-start(bf16[1,32,768]{2,1,0:T(8,128)(2,1)S(1)} %get-tuple-element.32), channel_id=1, source_target_pairs={{0,30},{2,28},{4,26},{6,24},{8,22},{10,20},{12,18},{14,16},{16,14}... | collective-permute-start | bytes 147464 | tf_op jit(solution)/shard_map/ppermute | solution.py:73
  120.8 18.9 %all-to-all-start.1 = ((bf16[16,32,768]{2,1,0:T(8,128)(2,1)}), bf16[16,32,768]{2,1,0:T(8,128)(2,1)S(1)}, u32[]{:S(2)}, u32[]{:S(2)}) async-start(bf16[16,32,768]{2,1,0:T(8,128)(2,1)} %bitcast.108), calls=%async_computation.2 | async-start | bytes 1572864 | tf_op jit(solution)/shard_map/all_to_all | solution.py:153
  124.4 63.4 %all-gather.7.cloned.1.call-start = ((), (), s32[]{:S(2)}) async-start(), calls=%async_computation.7 | async-start | bytes 2359296 | tf_op jit(solution)/shard_map/all_gather | solution.py:166
  140.6 68.4 %reduce-scatter.7.cloned.1.call-start = ((), (), s32[]{:S(2)}) async-start(), calls=%async_computation.6 | async-start | bytes 2359296 | tf_op jit(solution)/shard_map/reduce_scatter | solution.py:175
  178.9 23.8 %slice-start = ((s8[4718592]{0:T(1024)(128)(4,1)}), s8[524288]{0:T(1024)(128)(4,1)S(1)}, s32[]{:S(2)}) async-start(s8[4718592]{0:T(1024)(128)(4,1)} %bitcast.115), calls=%async_computation.11 | async-start | bytes 1048576
  187.4 29.7 %reduce-scatter.9.cloned.1.call-start = ((), (), s32[]{:S(2)}) async-start(), calls=%async_computation.8 | async-start | bytes 2359296 | tf_op jit(solution)/shard_map/reduce_scatter | solution.py:185
  187.9 14.8 %slice-start.1 = ((s8[4718592]{0:T(1024)(128)(4,1)}), s8[4194304]{0:T(1024)(128)(4,1)S(1)}, s32[]{:S(2)}) async-start(s8[4718592]{0:T(1024)(128)(4,1)} %bitcast.115), calls=%async_computation.12 | async-start | bytes 8388608
  209.0 22.5 %all-to-all-start = ((bf16[16,32,768]{2,1,0:T(8,128)(2,1)}), bf16[16,32,768]{2,1,0:T(8,128)(2,1)S(1)}, u32[]{:S(2)}, u32[]{:S(2)}) async-start(bf16[16,32,768]{2,1,0:T(8,128)(2,1)} %bitcast.110), calls=%async_computation.1 | async-start | bytes 1572864 | tf_op jit(solution)/shard_map/all_to_all | solution.py:191
  231.5 22.9 %all-to-all-start.2 = ((bf16[16,32,768]{2,1,0:T(8,128)(2,1)}), bf16[16,32,768]{2,1,0:T(8,128)(2,1)S(1)}, u32[]{:S(2)}, u32[]{:S(2)}) async-start(bf16[16,32,768]{2,1,0:T(8,128)(2,1)} %bitcast.109), calls=%async_computation.4 | async-start | bytes 1572864 | tf_op jit(solution)/shard_map/all_to_all | solution.py:204
  235.9 135.1 %all-reduce.10.cloned.1.call-start = ((), (), s32[]{:S(2)}) async-start(), calls=%async_computation.9 | async-start | bytes 196608 | tf_op jit(solution)/shard_map/psum | solution.py:267
  248.9 14.5 %copy-start.4 = (f32[197,768]{1,0:T(8,128)S(1)}, f32[197,768]{1,0:T(8,128)}, u32[]{:S(2)}) copy-start(f32[197,768]{1,0:T(8,128)} %copy-done.3) | copy-start | bytes 1815556
  248.9 14.5 %copy-start.27 = (bf16[768,32]{0,1:T(8,128)(2,1)S(1)}, bf16[768,32]{0,1:T(8,128)(2,1)}, u32[]{:S(2)}) copy-start(bf16[768,32]{0,1:T(8,128)(2,1)} %param.19) | copy-start | bytes 147460
  248.9 309.2 %all-reduce.12.cloned.1.call-start = ((), (), s32[]{:S(2)}) async-start(), calls=%async_computation.10 | async-start | bytes 9437184 | tf_op jit(solution)/shard_map/psum | solution.py:266
  257.1 10.8 %copy-start.10 = (bf16[197,768]{1,0:T(8,128)(2,1)S(1)}, bf16[197,768]{1,0:T(8,128)(2,1)}, u32[]{:S(2)}) copy-start(bf16[197,768]{1,0:T(8,128)(2,1)} %param.23) | copy-start | bytes 907780
  268.0 10.6 %copy-start.14 = (bf16[2,197,6,1,64]{1,4,2,0,3:T(8,128)(2,1)S(1)}, bf16[2,197,6,1,64]{1,4,2,0,3:T(8,128)(2,1)}, u32[]{:S(2)}) copy-start(bf16[2,197,6,1,64]{1,4,2,0,3:T(8,128)(2,1)} %copy-done.13) | copy-start | bytes 907780
  290.0 10.0 %copy-start.24 = (bf16[394,1152]{0,1:T(8,128)(2,1)S(1)}, bf16[394,1152]{0,1:T(8,128)(2,1)}, u32[]{:S(2)}) copy-start(bf16[394,1152]{0,1:T(8,128)(2,1)} %convert_element_type.115) | copy-start | bytes 2723332
  305.4 14.6 %copy-start.6 = (bf16[197,768]{1,0:T(8,128)(2,1)S(1)}, bf16[197,768]{1,0:T(8,128)(2,1)}, u32[]{:S(2)}) copy-start(bf16[197,768]{1,0:T(8,128)(2,1)} %param.12) | copy-start | bytes 907780
  305.4 14.6 %copy-start.29 = (f32[768]{0:T(1024)S(1)}, f32[768]{0:T(1024)}, u32[]{:S(2)}) copy-start(f32[768]{0:T(1024)} %param.13) | copy-start | bytes 9220
  305.4 14.6 %copy-start.32 = (f32[197]{0:T(256)S(1)}, f32[197]{0:T(256)}, u32[]{:S(2)}) copy-start(f32[197]{0:T(256)} %copy-done.31) | copy-start | bytes 2368
  305.4 14.9 %copy-start.37 = (f32[197]{0:T(256)S(1)}, f32[197]{0:T(256)}, u32[]{:S(2)}) copy-start(f32[197]{0:T(256)} %copy-done.36) | copy-start | bytes 2368
  305.4 14.9 %copy-start.35 = (f32[197]{0:T(256)S(1)}, f32[197]{0:T(256)}, u32[]{:S(2)}) copy-start(f32[197]{0:T(256)} %copy-done.34) | copy-start | bytes 2368
  305.5 55.0 %copy-start.8 = (f32[197,768]{1,0:T(8,128)S(1)}, f32[197,768]{1,0:T(8,128)}, u32[]{:S(2)}) copy-start(f32[197,768]{1,0:T(8,128)} %copy-done.7) | copy-start | bytes 1815556
  305.5 12.5 %collective-permute-start.16 = (bf16[3,768]{1,0:T(4,128)(2,1)S(1)}, bf16[3,768]{1,0:T(4,128)(2,1)S(1)}, u32[]{:S(2)}, u32[]{:S(2)}) collective-permute-start(bf16[3,768]{1,0:T(4,128)(2,1)S(1)} %slice.34), channel_id=1, source_target_pairs={{0,1},{2,3},{4,5},{6,7},{8,9},{10,11},{12,13},{14,15},{16,17},{18,... | collective-permute-start | bytes 13832
  (20 other events, 53.8 us)
Sparse Core Ops, SparseCore 0:
  117.5 6.6 all-gather.4
  140.7 8.4 all-gather.6
  187.5 7.7 reduce-scatter.6
  209.1 8.0 reduce-scatter.8
  249.0 121.8 all-reduce.9
  377.1 180.9 all-reduce.11
